TPU v7x, 256 devices: a whole 4x4x8 slice. The times are simulated.
256 devices in a mesh: mem: 32 (over z, x), space: 8 (over y, core).
Axes of the slice: x: 4, y: 4, z: 8, core: 2. Of those that a mesh axis runs over, the one named last changes fastest.
Arguments:
- params: float32 [256, 16, 16, 384], P('mem', 'space'), may hold values from -6 to 6
- start_field: float32 [16, 16, 384], P('space'), may hold values from -6 to 6
- obs_index: int32 [8192], P('space'), may hold values from 0 to 12287
- observed: float32 [8192], P('space'), may hold values from -16 to 16
- obs_noise: float32 [256, 8192], P('mem', 'space'), may hold values from -6 to 6
Outputs:
- updated: float32 [256, 16, 16, 384], P('mem', 'space')
- predicted: float32 [256, 8192], P('mem', 'space')
Inputs may be any that keep to these rules, and one draw needn't show every extreme that they name: `obs_index`: each entry is the position, row by level by column, of a cell within the 2 rows of its own block; cells may repeat.
All inputs are finite; a program needn't handle non-finite values.
Results may differ from a plain program's by a relative error of at most 0.00025.
Values sent between devices are 32-bit elements; how exact they have to be, the bound alone decides.
A program may use at most 64 MiB of HBM per device.

v0:
```python
import jax
import jax.numpy as jnp
from jax import lax
from jax.sharding import PartitionSpec as P

obs_variance = 0.02
step_weight = 0.25


def extended(cells, sides, width):
    for axis, dim in sides:
        count = lax.axis_size(axis)
        ends = count - 1
        head = lax.slice_in_dim(cells, 0, width, axis=dim)
        tail = lax.slice_in_dim(cells, cells.shape[dim] - width, cells.shape[dim], axis=dim)
        cells = jnp.concatenate(
            [
                lax.ppermute(tail, axis, [(i, (i + 1) % count) for i in range(ends)]),
                cells,
                lax.ppermute(head, axis, [((i + 1) % count, i) for i in range(ends)]),
            ],
            axis=dim,
        )
    return cells


def advance(padded, diffusivity):
    center = padded[:, 1:-1]
    col_padded = jnp.pad(center, ((0, 0), (0, 0), (0, 0), (1, 1)))
    laplace_sum = (
        padded[:, 2:] + padded[:, :-2] + col_padded[..., 2:] + col_padded[..., :-2] - 4.0 * center
    )
    return center + step_weight * diffusivity * laplace_sum


def product(left, right):
    return jnp.dot(left, right, precision=lax.Precision.HIGHEST, preferred_element_type=jnp.float32)


def per_device(params, start_field, obs_index, observed, obs_noise):
    mem_local = params.shape[0]
    members = mem_local * lax.axis_size("mem")
    nobs_all = observed.shape[0] * lax.axis_size("space")
    diffusivity = 0.1 + 0.8 * jax.nn.sigmoid(params)
    start_pad = extended(start_field, (("space", 0),), 1)
    first_step = advance(start_pad[None], diffusivity)
    first_pad = extended(first_step, (("space", 1),), 1)
    second = advance(first_pad, diffusivity)
    predicted = second.reshape(mem_local, -1)[:, obs_index]
    misfit = observed[None, :] + obs_noise - predicted
    pred_all, misfit_all = (
        lax.all_gather(predicted, "mem", axis=0, tiled=True),
        lax.all_gather(misfit, "mem", axis=0, tiled=True),
    )
    spread_all = pred_all - jnp.mean(pred_all, axis=0)
    lead_row = lax.axis_index("mem") * mem_local
    spread_own = lax.dynamic_slice_in_dim(spread_all, lead_row, mem_local, 0)
    rows_aa, rows_ad = lax.psum(
        (product(spread_own, spread_all.T), product(spread_own, misfit_all.T)), "space"
    )
    gram_aa, gram_ad = (
        lax.all_gather(rows_aa, "mem", axis=0, tiled=True),
        lax.all_gather(rows_ad, "mem", axis=0, tiled=True),
    )
    factor = jnp.linalg.cholesky(
        gram_aa / nobs_all + obs_variance * jnp.eye(members, dtype=jnp.float32)
    )
    weights = jax.scipy.linalg.cho_solve((factor, True), gram_ad / nobs_all)
    flat_params = params.reshape(mem_local, -1)
    own_cols = lax.dynamic_slice_in_dim(weights, lead_row, mem_local, 1)
    shifted = product(own_cols.T, lax.all_gather(flat_params, "mem", axis=0, tiled=True))
    updated = params + shifted.reshape(params.shape)
    return (updated, predicted)


def solution(mesh):
    in_specs = (
        P("mem", "space", None, None),
        P("space", None, None),
        P("space"),
        P("space"),
        P("mem", "space"),
    )
    out_specs = (P("mem", "space", None, None), P("mem", "space"))
    return jax.shard_map(
        per_device, mesh=mesh, in_specs=in_specs, out_specs=out_specs, check_vma=False
    )
```

profile of v0, /device:TPU:2, one launch (start us, length us, event | category | flops | bytes accessed | tf_op | source)
XLA Modules:
  0.0 396.2 jit_solution(32803249334153336)
XLA Ops:
  7.2 0.8 fusion.36
  8.0 1.7 collective-permute-start
  9.7 1.3 collective-permute-start.1
  11.0 3.1 collective-permute-done.1
  14.2 0.8 maximum_bitcast_fusion
  15.1 1.1 multiply_add_fusion
  16.2 1.3 collective-permute-start.2
  17.5 5.1 %collective-permute-start.3 = (f32[8,1,16,384]{3,2,1,0:T(8,128)S(1)}, f32[8,1,16,384]{3,2,1,0:T(8,128)S(1)}, u32[]{:S(2)}, u32[]{:S(2)}) collective-permute-start(f32[8,1,16,384]{3,2,1,0:T(8,128)S(1)} %get-tuple-element.39), channel_id=1, source_target_pairs={{0,1},{1,2},{2,3},{3,4},{4,5},{5,6},{6,7},{8,9},{9,10},{10,11},{11... | collective-permute-start | bytes 589832 | tf_op jit(solution)/shard_map/ppermute | solution.py:18
  22.7 0.7 fusion.29
  23.4 0.3 collective-permute-done.3
  23.7 1.3 fusion.4
  25.0 4.0 %copy.33 = f32[8,2,16,384]{0,3,2,1:T(8,128)} copy(f32[8,2,16,384]{3,2,1,0:T(8,128)S(1)} %fusion.4) | data formatting | bytes 786432 | tf_op jit(solution)/shard_map/add | solution.py:33
  29.0 5.6 %gather_fusion = f32[1024,8]{1,0:T(8,128)S(1)} fusion(f32[8,12288]{0,1:T(8,128)} %bitcast.50, s32[1024]{0:T(1024)S(1)} %fusion.29), kind=kCustom, calls=%fused_computation | custom fusion | bytes 69632 | tf_op jit(solution)/shard_map/gather | solution.py:49
  34.6 0.8 copy.34
  35.5 1.4 add_subtract_fusion
  36.9 2.0 copy.46
  39.0 78.9 %all-gather.9.cloned.1.call-done = f32[256,1024]{1,0:T(8,128)} async-done(((f32[8,1024]{1,0:T(8,128)}), f32[256,1024]{1,0:T(8,128)}) %all-gather.9.cloned.1.call-update) | async-done | bytes 1048592 | tf_op jit(solution)/shard_map/all_gather | solution.py:52
  117.8 1.3 reduce_sum.9
  119.1 1.3 broadcast_subtract_fusion
  120.5 0.9 fusion.27
  121.4 72.9 %all-gather.5.cloned.1.call-done = f32[256,1024]{1,0:T(8,128)} async-done(((f32[8,1024]{1,0:T(8,128)}), f32[256,1024]{1,0:T(8,128)}) %all-gather.5.cloned.1.call-update) | async-done | bytes 1048592 | tf_op jit(solution)/shard_map/all_gather | solution.py:53
  194.3 2.1 fusion.25
  196.4 23.6 %all-reduce.3 = (f32[8,256]{1,0:T(8,128)S(1)}, f32[8,256]{1,0:T(8,128)S(1)}) all-reduce(f32[8,256]{1,0:T(8,128)S(1)} %fusion.25, f32[8,256]{1,0:T(8,128)S(1)} %fusion.27), channel_id=1, replica_groups=mesh['mem'=32,'space'=8] {'space'}, use_global_device_ids=true, to_apply=%region_6.7 | all-reduce | flops 4096 | bytes 32768 | tf_op jit(solution)/shard_map/psum | solution.py:58
  220.0 48.8 %all_gather.16 = f32[256,256]{1,0:T(8,128)S(1)} all-gather(f32[8,256]{1,0:T(8,128)S(1)} %get-tuple-element.35), channel_id=1, replica_groups=mesh['mem'=32,'space'=8] {'mem'}, dimensions={0}, use_global_device_ids=true | all-gather | bytes 270336 | tf_op jit(solution)/shard_map/all_gather | solution.py:62
  268.8 0.1 copy.35
  269.0 0.1 copy.36
  269.2 11.7 %cholesky.49 = f32[128,128]{1,0:T(8,128)S(1)} custom-call(f32[128,128]{1,0:T(8,128)S(1)} %cholesky.115), custom_call_target="Cholesky" | custom-call | tf_op jit(solution)/shard_map/jit(cholesky)/cholesky | solution.py:65
  281.0 9.8 %custom-call.18 = f32[1,128,128]{1,2,0:T(8,128)S(1)} custom-call(f32[1,128,128]{2,1,0:T(8,128)S(1)} %get-tuple-element.43), custom_call_target="InvertDiagBlocksLowerTriangular" | custom-call | tf_op jit(solution)/shard_map/jit(cholesky)/cholesky | solution.py:65
  290.9 0.2 fusion.12
  291.2 0.3 convolution_subtract_fusion.2
  291.4 11.7 %cholesky.103 = f32[128,128]{1,0:T(8,128)S(1)} custom-call(f32[128,128]{1,0:T(8,128)S(1)} %convolution_subtract_fusion.2), custom_call_target="Cholesky" | custom-call | tf_op jit(solution)/shard_map/jit(cholesky)/cholesky | solution.py:65
  303.3 0.6 compare_reduce_fusion
  305.3 4.2 %while.1 = (s32[]{:T(128)}, f32[256,256]{0,1:T(8,128)S(1)}, s32[2,2]{1,0:T(2,128)S(1)}, f32[2,128,128]{2,1,0:T(8,128)S(1)}, s32[]{:T(128)}) while((s32[]{:T(128)}, f32[256,256]{0,1:T(8,128)S(1)}, s32[2,2]{1,0:T(2,128)S(1)}, f32[2,128,128]{2,1,0:T(8,128)S(1)}, s32[]{:T(128)}) %tuple.33), condition=%wide.while_cond, body=%wide.while_body.sunk | while | flops 2 | bytes 393321 | solution.py:68
  305.5 0.6 fusion.48
  306.1 1.3 dynamic-slice.7
  307.5 0.6 fusion.48
  308.1 1.3 dynamic-slice.7
  309.5 19.7 %custom-call.19 = f32[2,128,128]{1,2,0:T(8,128)S(1)} custom-call(f32[2,128,128]{2,1,0:T(8,128)S(1)} %get-tuple-element.9), custom_call_target="InvertDiagBlocksLowerTriangular" | custom-call | tf_op jit(solution)/shard_map/jit(_cho_solve)/triangular_solve | solution.py:68
  329.2 48.6 %all_gather.18 = f32[256,256]{1,0:T(8,128)S(1)} all-gather(f32[8,256]{1,0:T(8,128)S(1)} %get-tuple-element.34), channel_id=1, replica_groups=mesh['mem'=32,'space'=8] {'mem'}, dimensions={0}, use_global_device_ids=true | all-gather | bytes 270336 | tf_op jit(solution)/shard_map/all_gather | solution.py:63
  377.8 0.1 copy.41
  377.9 0.3 fusion.10
  378.2 0.4 convolution_subtract_fusion.1
  378.6 0.3 fusion.17
  379.0 0.3 fusion.16
  379.2 0.3 convolution_subtract_fusion
  379.5 0.3 fusion.15
  379.8 9.0 %fusion.8 = f32[8,12288]{1,0:T(8,128)S(1)} fusion(f32[256,12288]{1,0:T(8,128)} %all-gather.7.cloned.1.call-done, s32[]{:T(128)S(6)} %select_n.12, f32[128,256]{1,0:T(8,128)S(1)} %fusion.15, f32[128,256]{1,0:T(8,128)S(1)} %fusion.16), kind=kOutput, calls=%fused_computation.29 | convolution fusion | flops 301991936 | bytes 13238276 | tf_op jit(solution)/shard_map/dot_general | solution.py:37
  388.8 0.8 copy_add_fusion
  (37 shorter events, 1.1 us)
Async XLA Ops:
  7.2 110.7 %all-gather.9.cloned.1.call-start = ((), (), s32[]{:S(2)}) async-start(), calls=%async_computation.2 | async-start | bytes 1081344 | tf_op jit(solution)/shard_map/all_gather | solution.py:52
  8.0 3.0 collective-permute-start
  9.7 4.5 %collective-permute-start.1 = (f32[1,16,384]{2,1,0:T(8,128)S(1)}, f32[1,16,384]{2,1,0:T(8,128)S(1)}, u32[]{:S(2)}, u32[]{:S(2)}) collective-permute-start(f32[1,16,384]{2,1,0:T(8,128)S(1)} %get-tuple-element.45), channel_id=1, source_target_pairs={{1,0},{2,1},{3,2},{4,3},{5,4},{6,5},{7,6},{9,8},{10,9},{11,10},{12... | collective-permute-start | bytes 73736 | tf_op jit(solution)/shard_map/ppermute | solution.py:20
  16.2 7.1 %collective-permute-start.2 = (f32[8,1,16,384]{3,2,1,0:T(8,128)S(1)}, f32[8,1,16,384]{3,2,1,0:T(8,128)S(1)}, u32[]{:S(2)}, u32[]{:S(2)}) collective-permute-start(f32[8,1,16,384]{3,2,1,0:T(8,128)S(1)} %get-tuple-element.38), channel_id=1, source_target_pairs={{1,0},{2,1},{3,2},{4,3},{5,4},{6,5},{7,6},{9,8},{10,9},{11,10},{12... | collective-permute-start | bytes 589832 | tf_op jit(solution)/shard_map/ppermute | solution.py:20
  17.5 6.1 %collective-permute-start.3 = (f32[8,1,16,384]{3,2,1,0:T(8,128)S(1)}, f32[8,1,16,384]{3,2,1,0:T(8,128)S(1)}, u32[]{:S(2)}, u32[]{:S(2)}) collective-permute-start(f32[8,1,16,384]{3,2,1,0:T(8,128)S(1)} %get-tuple-element.39), channel_id=1, source_target_pairs={{0,1},{1,2},{2,3},{3,4},{4,5},{5,6},{6,7},{8,9},{9,10},{10,11},{11... | collective-permute-start | bytes 589832 | tf_op jit(solution)/shard_map/ppermute | solution.py:18
  35.4 158.9 %all-gather.5.cloned.1.call-start = ((), (), s32[]{:S(2)}) async-start(), calls=%async_computation | async-start | bytes 1081344 | tf_op jit(solution)/shard_map/all_gather | solution.py:53
  36.9 342.9 %all-gather.7.cloned.1.call-start = ((), (), s32[]{:S(2)}) async-start(), calls=%async_computation.1 | async-start | bytes 12976128 | tf_op jit(solution)/shard_map/all_gather | solution.py:71
  121.4 267.4 %copy-start = (f32[8,2,16,384]{3,2,1,0:T(8,128)S(1)}, f32[8,2,16,384]{3,2,1,0:T(8,128)}, u32[]{:S(2)}) copy-start(f32[8,2,16,384]{3,2,1,0:T(8,128)} %param.5) | copy-start | bytes 1179652
Sparse Core Ops, SparseCore 0:
  35.5 82.2 all-gather.8
  120.4 73.8 all-gather.4
  197.5 116.4 all-gather.6
where the time goes:
time: 397 us; the launch traced here: 396 us
  waiting for transfers between devices  155 us (39%)
  blocking collectives  121 us (30%)
  other arithmetic  62.7 us (16%)
  local copies, waits for them, and re-layouts  17.9 us (5%)
  between operations  15.2 us (4%)
  matrix products  14.4 us (4%)
  starting transfers between devices  9.53 us (2%)
    all_gather x1, waiting for transfers between devices, per_device(): lax.all_gather(predicted, 'mem', axis=0, tiled=True)  78.9 us
    all_gather x1, waiting for transfers between devices, per_device(): lax.all_gather(misfit, 'mem', axis=0, tiled=True)  72.9 us
    all_gather x1, blocking collectives, per_device(): lax.all_gather(rows_aa, 'mem', axis=0, tiled=True)  48.8 us
    all_gather x1, blocking collectives, per_device(): lax.all_gather(rows_ad, 'mem', axis=0, tiled=True)  48.6 us
    another operation x6, other arithmetic, per_device(): jnp.linalg.cholesky(gram_aa / nobs_all + obs_variance * jnp.eye(members,...  34 us
    psum x1, blocking collectives, per_device(): lax.psum((product(spread_own, spread_all.T), product(spread_own, misfit_a...  23.6 us
    another operation x3, other arithmetic, per_device(): weights = jax.scipy.linalg.cho_solve((factor, True), gram_ad / nobs_all)  19.7 us
    dot_general x3, matrix products, product(): jnp.dot(left, right, precision=lax.Precision.HIGHEST, preferred_element_t...  12.1 us
  transfers between devices with their start and end apart: 7, of which 4 were waited for; matrix products, arithmetic and copies ran while one was open for 18% of the time, Pallas kernels for 0%

commit v1 on v0

--- a/solution.py
+++ b/solution.py
@@ -2,6 +2,7 @@
 import jax.numpy as jnp
 from jax import lax
 from jax.sharding import PartitionSpec as P
+from jax.lax import all_to_all, axis_size
 
 obs_variance = 0.02
 step_weight = 0.25
@@ -58,9 +59,12 @@
     rows_aa, rows_ad = lax.psum(
         (product(spread_own, spread_all.T), product(spread_own, misfit_all.T)), "space"
     )
+    mark_thing = lambda in_array, dev_axis: jnp.concatenate(
+        all_to_all(jnp.stack([in_array] * axis_size(dev_axis)), dev_axis, 0, 0), axis=0
+    )
     gram_aa, gram_ad = (
         lax.all_gather(rows_aa, "mem", axis=0, tiled=True),
-        lax.all_gather(rows_ad, "mem", axis=0, tiled=True),
+        mark_thing(rows_ad, "mem"),
     )
     factor = jnp.linalg.cholesky(
         gram_aa / nobs_all + obs_variance * jnp.eye(members, dtype=jnp.float32)

time: 397 us -> 358 us (0.902)
  blocking collectives: 121 us -> 72.4 us
  starting transfers between devices: 9.53 us -> 17.8 us
    all_gather x1 -> x0, blocking collectives: 48.6 us -> none  [per_device(): lax.all_gather(rows_ad, 'mem', axis=0, tiled=True)]
    all_to_all x0 -> x1, starting transfers between devices: none -> 8.28 us  [per_device(): all_to_all(jnp.stack([in_array] * axis_size(dev_axis)), dev_axis, 0, 0)]
  transfers between devices with their start and end apart: 7 -> 8, of which waited for: 4 -> 4; matrix products, arithmetic and copies ran while one was open for 18% -> 20% of each run, Pallas kernels for 0% -> 0%
where the time goes in v1:
time: 358 us; the launch traced here: 357 us
  waiting for transfers between devices  155 us (43%)
  blocking collectives  72.4 us (20%)
  other arithmetic  62.7 us (18%)
  local copies, waits for them, and re-layouts  18.9 us (5%)
  starting transfers between devices  17.8 us (5%)
  between operations  15.3 us (4%)
  matrix products  14.3 us (4%)
    all_gather x1, waiting for transfers between devices, per_device(): lax.all_gather(predicted, 'mem', axis=0, tiled=True)  78.8 us
    all_gather x1, waiting for transfers between devices, per_device(): lax.all_gather(misfit, 'mem', axis=0, tiled=True)  72.9 us
    all_gather x1, blocking collectives, per_device(): lax.all_gather(rows_aa, 'mem', axis=0, tiled=True)  48.8 us
    another operation x6, other arithmetic, per_device(): jnp.linalg.cholesky(gram_aa / nobs_all + obs_variance * jnp.eye(members,...  34 us
    psum x1, blocking collectives, per_device(): lax.psum((product(spread_own, spread_all.T), product(spread_own, misfit_a...  23.6 us
    another operation x3, other arithmetic, per_device(): weights = jax.scipy.linalg.cho_solve((factor, True), gram_ad / nobs_all)  19.7 us
    dot_general x3, matrix products, product(): jnp.dot(left, right, precision=lax.Precision.HIGHEST, preferred_element_t...  12.1 us
    all_to_all x1, starting transfers between devices, per_device(): all_to_all(jnp.stack([in_array] * axis_size(dev_axis)), dev_axis, 0, 0)  8.28 us
  transfers between devices with their start and end apart: 8, of which 4 were waited for; matrix products, arithmetic and copies ran while one was open for 20% of the time, Pallas kernels for 0%

profile of v1, /device:TPU:2, one launch (start us, length us, event | category | flops | bytes accessed | tf_op | source)
XLA Modules:
  0.0 356.8 jit_solution(18321428292436131652)
XLA Ops:
  7.2 0.8 fusion.35
  8.0 1.7 collective-permute-start
  9.7 1.3 collective-permute-start.1
  11.0 3.1 collective-permute-done.1
  14.2 0.8 maximum_bitcast_fusion
  15.1 1.1 multiply_add_fusion
  16.2 1.3 collective-permute-start.2
  17.5 5.1 %collective-permute-start.3 = (f32[8,1,16,384]{3,2,1,0:T(8,128)S(1)}, f32[8,1,16,384]{3,2,1,0:T(8,128)S(1)}, u32[]{:S(2)}, u32[]{:S(2)}) collective-permute-start(f32[8,1,16,384]{3,2,1,0:T(8,128)S(1)} %get-tuple-element.39), channel_id=1, source_target_pairs={{0,1},{1,2},{2,3},{3,4},{4,5},{5,6},{6,7},{8,9},{9,10},{10,11},{11... | collective-permute-start | bytes 589832 | tf_op jit(solution)/shard_map/ppermute | solution.py:19
  22.7 0.7 fusion.28
  23.4 0.3 collective-permute-done.3
  23.7 1.3 fusion.4
  25.0 4.2 %copy.31 = f32[8,2,16,384]{0,3,2,1:T(8,128)} copy(f32[8,2,16,384]{3,2,1,0:T(8,128)S(1)} %fusion.4) | data formatting | bytes 786432 | tf_op jit(solution)/shard_map/add | solution.py:34
  29.2 5.6 %gather_fusion = f32[1024,8]{1,0:T(8,128)S(1)} fusion(f32[8,12288]{0,1:T(8,128)} %bitcast.57, s32[1024]{0:T(1024)S(1)} %fusion.28), kind=kCustom, calls=%fused_computation | custom fusion | bytes 69632 | tf_op jit(solution)/shard_map/gather | solution.py:50
  34.8 0.8 copy.32
  35.6 1.4 add_subtract_fusion
  37.1 2.0 copy.41
  39.2 78.8 %all-gather.9.cloned.1.call-done = f32[256,1024]{1,0:T(8,128)} async-done(((f32[8,1024]{1,0:T(8,128)}), f32[256,1024]{1,0:T(8,128)}) %all-gather.9.cloned.1.call-update) | async-done | bytes 1048592 | tf_op jit(solution)/shard_map/all_gather | solution.py:53
  118.0 1.3 reduce_sum.9
  119.3 1.3 broadcast_subtract_fusion
  120.7 0.9 fusion.26
  121.6 72.9 %all-gather.5.cloned.1.call-done = f32[256,1024]{1,0:T(8,128)} async-done(((f32[8,1024]{1,0:T(8,128)}), f32[256,1024]{1,0:T(8,128)}) %all-gather.5.cloned.1.call-update) | async-done | bytes 1048592 | tf_op jit(solution)/shard_map/all_gather | solution.py:54
  194.5 2.1 fusion.24
  196.6 23.6 %all-reduce.3 = (f32[8,256]{1,0:T(8,128)S(1)}, f32[8,256]{1,0:T(8,128)S(1)}) all-reduce(f32[8,256]{1,0:T(8,128)S(1)} %fusion.24, f32[8,256]{1,0:T(8,128)S(1)} %fusion.26), channel_id=1, replica_groups=mesh['mem'=32,'space'=8] {'space'}, use_global_device_ids=true, to_apply=%region_6.7 | all-reduce | flops 4096 | bytes 32768 | tf_op jit(solution)/shard_map/psum | solution.py:59
  220.2 48.8 %all_gather.13 = f32[256,256]{1,0:T(8,128)S(1)} all-gather(f32[8,256]{1,0:T(8,128)S(1)} %get-tuple-element.35), channel_id=1, replica_groups=mesh['mem'=32,'space'=8] {'mem'}, dimensions={0}, use_global_device_ids=true | all-gather | bytes 270336 | tf_op jit(solution)/shard_map/all_gather | solution.py:66
  269.0 0.1 copy.33
  269.2 0.1 copy.34
  269.4 11.7 %cholesky.49 = f32[128,128]{1,0:T(8,128)S(1)} custom-call(f32[128,128]{1,0:T(8,128)S(1)} %cholesky.115), custom_call_target="Cholesky" | custom-call | tf_op jit(solution)/shard_map/jit(cholesky)/cholesky | solution.py:69
  281.2 9.8 %custom-call.18 = f32[1,128,128]{1,2,0:T(8,128)S(1)} custom-call(f32[1,128,128]{2,1,0:T(8,128)S(1)} %get-tuple-element.43), custom_call_target="InvertDiagBlocksLowerTriangular" | custom-call | tf_op jit(solution)/shard_map/jit(cholesky)/cholesky | solution.py:69
  291.0 0.2 fusion.11
  291.3 0.3 convolution_subtract_fusion.2
  291.6 11.7 %cholesky.103 = f32[128,128]{1,0:T(8,128)S(1)} custom-call(f32[128,128]{1,0:T(8,128)S(1)} %convolution_subtract_fusion.2), custom_call_target="Cholesky" | custom-call | tf_op jit(solution)/shard_map/jit(cholesky)/cholesky | solution.py:69
  303.5 0.7 stack.2
  304.2 8.3 %all-to-all-start = ((f32[32,8,256]{2,1,0:T(8,128)}), f32[32,8,256]{2,1,0:T(8,128)S(1)}, u32[]{:S(2)}, u32[]{:S(2)}) async-start(f32[32,8,256]{2,1,0:T(8,128)} %stack.2), calls=%async_computation | async-start | bytes 524288 | tf_op jit(solution)/shard_map/all_to_all | solution.py:63
  312.5 0.7 compare_reduce_fusion
  314.6 4.2 %while.1 = (s32[]{:T(128)}, f32[256,256]{0,1:T(8,128)S(1)}, s32[2,2]{1,0:T(2,128)S(1)}, f32[2,128,128]{2,1,0:T(8,128)S(1)}, s32[]{:T(128)}) while((s32[]{:T(128)}, f32[256,256]{0,1:T(8,128)S(1)}, s32[2,2]{1,0:T(2,128)S(1)}, f32[2,128,128]{2,1,0:T(8,128)S(1)}, s32[]{:T(128)}) %tuple.33), condition=%wide.while_cond, body=%wide.while_body.sunk | while | flops 2 | bytes 393321 | solution.py:72
  314.6 0.6 fusion.47
  315.3 1.4 dynamic-slice.7
  316.8 0.6 fusion.47
  317.4 1.4 dynamic-slice.7
  318.9 19.7 %custom-call.19 = f32[2,128,128]{1,2,0:T(8,128)S(1)} custom-call(f32[2,128,128]{2,1,0:T(8,128)S(1)} %get-tuple-element.9), custom_call_target="InvertDiagBlocksLowerTriangular" | custom-call | tf_op jit(solution)/shard_map/jit(_cho_solve)/triangular_solve | solution.py:72
  338.6 0.3 fusion.10
  338.9 0.3 convolution_subtract_fusion.1
  339.2 0.3 fusion.16
  339.6 0.3 fusion.15
  339.8 0.3 convolution_subtract_fusion
  340.1 0.3 fusion.14
  340.4 9.0 %fusion.8 = f32[8,12288]{1,0:T(8,128)S(1)} fusion(f32[256,12288]{1,0:T(8,128)} %all-gather.7.cloned.1.call-done, s32[]{:T(128)S(6)} %select_n.12, f32[128,256]{1,0:T(8,128)S(1)} %fusion.14, f32[128,256]{1,0:T(8,128)S(1)} %fusion.15), kind=kOutput, calls=%fused_computation.29 | convolution fusion | flops 301991936 | bytes 13238276 | tf_op jit(solution)/shard_map/dot_general | solution.py:38
  349.4 0.8 copy_add_fusion
  (38 shorter events, 1.1 us)
Async XLA Ops:
  7.2 110.8 %all-gather.9.cloned.1.call-start = ((), (), s32[]{:S(2)}) async-start(), calls=%async_computation.3 | async-start | bytes 1081344 | tf_op jit(solution)/shard_map/all_gather | solution.py:53
  8.0 3.0 collective-permute-start
  9.7 4.5 %collective-permute-start.1 = (f32[1,16,384]{2,1,0:T(8,128)S(1)}, f32[1,16,384]{2,1,0:T(8,128)S(1)}, u32[]{:S(2)}, u32[]{:S(2)}) collective-permute-start(f32[1,16,384]{2,1,0:T(8,128)S(1)} %get-tuple-element.45), channel_id=1, source_target_pairs={{1,0},{2,1},{3,2},{4,3},{5,4},{6,5},{7,6},{9,8},{10,9},{11,10},{12... | collective-permute-start | bytes 73736 | tf_op jit(solution)/shard_map/ppermute | solution.py:21
  16.2 7.1 %collective-permute-start.2 = (f32[8,1,16,384]{3,2,1,0:T(8,128)S(1)}, f32[8,1,16,384]{3,2,1,0:T(8,128)S(1)}, u32[]{:S(2)}, u32[]{:S(2)}) collective-permute-start(f32[8,1,16,384]{3,2,1,0:T(8,128)S(1)} %get-tuple-element.38), channel_id=1, source_target_pairs={{1,0},{2,1},{3,2},{4,3},{5,4},{6,5},{7,6},{9,8},{10,9},{11,10},{12... | collective-permute-start | bytes 589832 | tf_op jit(solution)/shard_map/ppermute | solution.py:21
  17.5 6.1 %collective-permute-start.3 = (f32[8,1,16,384]{3,2,1,0:T(8,128)S(1)}, f32[8,1,16,384]{3,2,1,0:T(8,128)S(1)}, u32[]{:S(2)}, u32[]{:S(2)}) collective-permute-start(f32[8,1,16,384]{3,2,1,0:T(8,128)S(1)} %get-tuple-element.39), channel_id=1, source_target_pairs={{0,1},{1,2},{2,3},{3,4},{4,5},{5,6},{6,7},{8,9},{9,10},{10,11},{11... | collective-permute-start | bytes 589832 | tf_op jit(solution)/shard_map/ppermute | solution.py:19
  35.6 158.9 %all-gather.5.cloned.1.call-start = ((), (), s32[]{:S(2)}) async-start(), calls=%async_computation.1 | async-start | bytes 1081344 | tf_op jit(solution)/shard_map/all_gather | solution.py:54
  37.1 303.3 %all-gather.7.cloned.1.call-start = ((), (), s32[]{:S(2)}) async-start(), calls=%async_computation.2 | async-start | bytes 12976128 | tf_op jit(solution)/shard_map/all_gather | solution.py:75
  121.6 227.9 %copy-start = (f32[8,2,16,384]{3,2,1,0:T(8,128)S(1)}, f32[8,2,16,384]{3,2,1,0:T(8,128)}, u32[]{:S(2)}) copy-start(f32[8,2,16,384]{3,2,1,0:T(8,128)} %param.5) | copy-start | bytes 1179652
  304.2 34.4 %all-to-all-start = ((f32[32,8,256]{2,1,0:T(8,128)}), f32[32,8,256]{2,1,0:T(8,128)S(1)}, u32[]{:S(2)}, u32[]{:S(2)}) async-start(f32[32,8,256]{2,1,0:T(8,128)} %stack.2), calls=%async_computation | async-start | bytes 524288 | tf_op jit(solution)/shard_map/all_to_all | solution.py:63
Sparse Core Ops, SparseCore 0:
  35.7 82.2 all-gather.8
  120.6 73.8 all-gather.4
  197.6 119.2 all-gather.6
